TPU v7x, 32 devices: a whole 2x2x4 slice. The times are simulated.
32 devices in a mesh: tile: 8 (over z, x), freq: 4 (over y, core).
Axes of the slice: x: 2, y: 2, z: 4, core: 2. Of those that a mesh axis runs over, the one named last changes fastest.
Arguments:
- u_tiles: bfloat16 [4, 8, 8, 40, 1024], P('freq', 'tile'), may hold values from -0.3125 to 0.3125
- v_tiles: bfloat16 [4, 8, 8, 40, 1024], P('freq', None, 'tile'), may hold values from -0.1875 to 0.1875
- tile_ranks: int32 [4, 8, 8], P('freq'), may hold values from 4 to 40, as said below
- recorded: float32 [4, 8192, 128], P('freq', 'tile')
Outputs:
- model: float32 [4, 8192, 128], P('freq', 'tile')
- residual: float32 [4, 8192, 128], P('freq', 'tile')
- gradient: float32 [4, 8192, 128], P('freq', 'tile')
Inputs may be any that keep to these rules, and one draw needn't show every extreme that they name: `tile_ranks`: every draw holds a tile of rank 40 and a tile of rank 4.
All inputs are finite; a program needn't handle non-finite values.
Results may differ from a plain program's by a relative error of at most 0.02.
Values may be sent and summed in bfloat16 or wider, within the bound.
No kernel may reach another device: no remote copies, remote signals or barrier semaphores. Data moves between devices by JAX's collectives and lax.ppermute only.
A program may use at most 128 MiB of HBM per device.

v0:
```python
import jax
import jax.numpy as jnp
from jax import lax
from jax.sharding import PartitionSpec as P

ITERS = 2


def local(u_tiles, v_tiles, tile_ranks, recorded):
    count_freq, tile_dev, tiles_all, rank_pad, width = u_tiles.shape
    traces = recorded.shape[2]
    position = lax.axis_index("tile")
    levels = jnp.arange(rank_pad, dtype=jnp.int32)
    rank_rows = lax.dynamic_slice_in_dim(tile_ranks, position * tile_dev, tile_dev, 1)
    rank_cols = lax.dynamic_slice_in_dim(tile_ranks, position * tile_dev, tile_dev, 2)
    mask_rows = (levels < rank_rows[..., None]).astype(jnp.float32)[..., None]
    mask_cols = (levels < rank_cols[..., None]).astype(jnp.float32)[..., None]

    def apply_cols_part(coeffs):
        return jnp.einsum("fijrb,fijrs->fjbs", v_tiles, coeffs, preferred_element_type=jnp.float32)

    def column_coeffs(rounded):
        coeffs = jnp.einsum(
            "fijrb,fjbs->fijrs", v_tiles, rounded, preferred_element_type=jnp.float32
        )
        return (coeffs * mask_cols).astype(jnp.bfloat16)

    def row_coeffs(rounded):
        coeffs = jnp.einsum(
            "fijrb,fibs->fijrs", u_tiles, rounded, preferred_element_type=jnp.float32
        )
        return (coeffs * mask_rows).astype(jnp.bfloat16)

    def adjoint(field):
        rounded = field.astype(jnp.bfloat16).reshape(count_freq, tile_dev, width, traces)
        coeffs = row_coeffs(rounded)
        image = apply_cols_part(
            lax.all_to_all(coeffs, "tile", split_axis=2, concat_axis=1, tiled=True)
        )
        return image.reshape(count_freq, tile_dev * width, traces)

    def squares(field):
        return lax.psum(jnp.sum(field * field), ("tile", "freq"))

    model = jnp.zeros_like(recorded)
    resid = recorded
    gradient = adjoint(resid)
    direction = gradient
    gamma = squares(gradient)
    for iteration in range(ITERS):
        forward_rounded = direction.astype(jnp.bfloat16).reshape(
            count_freq, tile_dev, width, traces
        )
        forward_coeffs = column_coeffs(forward_rounded)
        forward_image = jnp.einsum(
            "fijrb,fijrs->fibs",
            u_tiles,
            lax.all_to_all(forward_coeffs, "tile", split_axis=1, concat_axis=2, tiled=True),
            preferred_element_type=jnp.float32,
        )
        image = forward_image.reshape(count_freq, tile_dev * width, traces)
        delta = squares(image)
        alpha = gamma / delta
        model = model + alpha * direction
        resid = resid - alpha * image
        gradient = adjoint(resid)
        gamma_new = squares(gradient)
        direction = gradient + gamma_new / gamma * direction
        gamma = gamma_new
    return (model, resid, gradient)


def solution(mesh):
    placed = (
        P("freq", "tile", None, None, None),
        P("freq", None, "tile", None, None),
        P("freq", None, None),
        P("freq", "tile", None),
    )
    return jax.shard_map(
        local,
        mesh=mesh,
        in_specs=placed,
        out_specs=(P("freq", "tile", None), P("freq", "tile", None), P("freq", "tile", None)),
        check_vma=False,
    )
```

profile of v0, /device:TPU:0, one launch (start us, length us, event | category | flops | bytes accessed | tf_op | source)
XLA Modules:
  0.0 193.8 jit_solution(4762774457426976636)
XLA Ops:
  0.7 0.7 copy-done.4
  1.5 2.2 %fusion.9 = bf16[1,1,8,40,128]{4,3,1,0,2:T(8,128)(2,1)} fusion(bf16[1,1,8,40,1024]{4,3,2,1,0:T(8,128)(2,1)} %param.4, f32[1,1024,128]{2,1,0:T(8,128)} %param.7, f32[8,40]{1,0:T(8,128)S(1)} %fusion.37), kind=kOutput, calls=%fused_computation.19 | convolution fusion | flops 84099072 | bytes 1262848 | tf_op jit(solution)/shard_map/fijrb,fibs->fijrs/dot_general | solution.py:29
  3.7 7.3 %all-to-all-start = ((bf16[1,1,8,40,128]{4,3,1,0,2:T(8,128)(2,1)}), bf16[1,1,8,40,128]{4,3,1,0,2:T(8,128)(2,1)S(1)}, u32[]{:S(2)}, u32[]{:S(2)}) async-start(bf16[1,1,8,40,128]{4,3,1,0,2:T(8,128)(2,1)} %fusion.9), calls=%async_computation | async-start | bytes 163840 | tf_op jit(solution)/shard_map/all_to_all | solution.py:38
  11.2 6.8 %all-to-all-done = bf16[1,1,8,40,128]{4,3,1,0,2:T(8,128)(2,1)S(1)} async-done(((bf16[1,1,8,40,128]{4,3,1,0,2:T(8,128)(2,1)}), bf16[1,1,8,40,128]{4,3,1,0,2:T(8,128)(2,1)S(1)}, u32[]{:S(2)}, u32[]{:S(2)}) %all-to-all-start) | async-done | bytes 81952 | tf_op jit(solution)/shard_map/all_to_all | solution.py:38
  18.0 1.0 multiply_reduce_fusion.3
  19.0 1.0 fusion.10
  20.0 3.5 %all-to-all-start.1 = ((bf16[1,8,1,40,128]{4,3,2,0,1:T(8,128)(2,1)}), bf16[1,8,1,40,128]{4,3,2,0,1:T(8,128)(2,1)S(1)}, u32[]{:S(2)}, u32[]{:S(2)}) async-start(bf16[1,8,1,40,128]{4,3,2,0,1:T(8,128)(2,1)} %fusion.10), calls=%async_computation.1 | async-start | bytes 163840 | tf_op jit(solution)/shard_map/all_to_all | solution.py:58
  23.7 6.7 %all-to-all-done.1 = bf16[1,8,1,40,128]{4,3,2,0,1:T(8,128)(2,1)S(1)} async-done(((bf16[1,8,1,40,128]{4,3,2,0,1:T(8,128)(2,1)}), bf16[1,8,1,40,128]{4,3,2,0,1:T(8,128)(2,1)S(1)}, u32[]{:S(2)}, u32[]{:S(2)}) %all-to-all-start.1) | async-done | bytes 81952 | tf_op jit(solution)/shard_map/all_to_all | solution.py:58
  30.4 1.0 multiply_reduce_fusion.2
  31.4 38.6 %all-reduce = (f32[]{:T(128)}, f32[]{:T(128)}) all-reduce(f32[]{:T(128)} %get-tuple-element.11, f32[]{:T(128)} %get-tuple-element.13), channel_id=1, replica_groups=mesh['tile'=8,'freq'=4] {'tile','freq'}, use_global_device_ids=true, to_apply=%region_1.0 | all-reduce | flops 2 | bytes 16 | tf_op jit(solution)/shard_map/psum | solution.py:43
  71.8 11.3 %all_to_all.20 = bf16[1,1,8,40,128]{4,3,1,0,2:T(8,128)(2,1)S(1)} all-to-all(bf16[1,1,8,40,128]{4,3,1,0,2:T(8,128)(2,1)S(1)} %fusion.8), channel_id=1, replica_groups=mesh['tile'=8,'freq'=4] {'tile'}, dimensions={2} | all-to-all | bytes 163840 | tf_op jit(solution)/shard_map/all_to_all | solution.py:38
  83.1 1.0 multiply_reduce_fusion.1
  84.1 38.6 %psum.30 = f32[]{:T(128)} all-reduce(f32[]{:T(128)} %get-tuple-element.15), channel_id=1, replica_groups=mesh['tile'=8,'freq'=4] {'tile','freq'}, use_global_device_ids=true, to_apply=%region_5.0 | all-reduce | flops 1 | bytes 8 | tf_op jit(solution)/shard_map/psum | solution.py:43
  124.1 0.4 fusion.11
  124.5 11.3 %all_to_all.21 = bf16[1,8,1,40,128]{4,3,2,0,1:T(8,128)(2,1)S(1)} all-to-all(bf16[1,8,1,40,128]{4,3,2,0,1:T(8,128)(2,1)S(1)} %fusion.11), channel_id=1, replica_groups=mesh['tile'=8,'freq'=4] {'tile'}, dimensions={1} | all-to-all | bytes 163840 | tf_op jit(solution)/shard_map/all_to_all | solution.py:58
  135.8 1.7 multiply_reduce_fusion
  137.5 38.7 %psum.31 = f32[]{:T(128)} all-reduce(f32[]{:T(128)} %get-tuple-element.17), channel_id=1, replica_groups=mesh['tile'=8,'freq'=4] {'tile','freq'}, use_global_device_ids=true, to_apply=%region_7.0 | all-reduce | flops 1 | bytes 8 | tf_op jit(solution)/shard_map/psum | solution.py:43
  177.6 1.3 bitcast_subtract_fusion
  179.0 1.0 fusion.7
  179.9 1.0 copy.22
  180.9 4.5 %all-to-all-start.4 = ((bf16[1,1,8,40,128]{4,3,1,0,2:T(8,128)(2,1)}), bf16[1,1,8,40,128]{4,3,1,0,2:T(8,128)(2,1)S(1)}, u32[]{:S(2)}, u32[]{:S(2)}) async-start(bf16[1,1,8,40,128]{4,3,1,0,2:T(8,128)(2,1)} %fusion.7), calls=%async_computation.4 | async-start | bytes 163840 | tf_op jit(solution)/shard_map/all_to_all | solution.py:38
  185.6 1.0 copy.21
  186.6 5.9 %all-to-all-done.4 = bf16[1,1,8,40,128]{4,3,1,0,2:T(8,128)(2,1)S(1)} async-done(((bf16[1,1,8,40,128]{4,3,1,0,2:T(8,128)(2,1)}), bf16[1,1,8,40,128]{4,3,1,0,2:T(8,128)(2,1)S(1)}, u32[]{:S(2)}, u32[]{:S(2)}) %all-to-all-start.4) | async-done | bytes 81952 | tf_op jit(solution)/shard_map/all_to_all | solution.py:38
  192.8 1.0 copy.23
  (17 shorter events, 1.3 us)
Async XLA Ops:
  0.6 17.4 %copy-start = (bf16[1,8,1,40,1024]{4,3,2,1,0:T(8,128)(2,1)S(1)}, bf16[1,8,1,40,1024]{4,3,2,1,0:T(8,128)(2,1)}, u32[]{:S(2)}) copy-start(bf16[1,8,1,40,1024]{4,3,2,1,0:T(8,128)(2,1)} %param.5) | copy-start | bytes 1966084
  0.6 0.8 copy-start.4
  3.7 14.3 %all-to-all-start = ((bf16[1,1,8,40,128]{4,3,1,0,2:T(8,128)(2,1)}), bf16[1,1,8,40,128]{4,3,1,0,2:T(8,128)(2,1)S(1)}, u32[]{:S(2)}, u32[]{:S(2)}) async-start(bf16[1,1,8,40,128]{4,3,1,0,2:T(8,128)(2,1)} %fusion.9), calls=%async_computation | async-start | bytes 163840 | tf_op jit(solution)/shard_map/all_to_all | solution.py:38
  19.0 4.5 %copy-start.3 = (f32[1,1024,128]{2,1,0:T(8,128)S(1)}, f32[1,1024,128]{2,1,0:T(8,128)}, u32[]{:S(2)}) copy-start(f32[1,1024,128]{2,1,0:T(8,128)} %param.7) | copy-start | bytes 1572868
  20.0 10.5 %copy-start.1 = (bf16[1,1,8,40,1024]{4,3,2,1,0:T(8,128)(2,1)S(1)}, bf16[1,1,8,40,1024]{4,3,2,1,0:T(8,128)(2,1)}, u32[]{:S(2)}) copy-start(bf16[1,1,8,40,1024]{4,3,2,1,0:T(8,128)(2,1)} %param.4) | copy-start | bytes 1966084
  20.0 10.4 %all-to-all-start.1 = ((bf16[1,8,1,40,128]{4,3,2,0,1:T(8,128)(2,1)}), bf16[1,8,1,40,128]{4,3,2,0,1:T(8,128)(2,1)S(1)}, u32[]{:S(2)}, u32[]{:S(2)}) async-start(bf16[1,8,1,40,128]{4,3,2,0,1:T(8,128)(2,1)} %fusion.10), calls=%async_computation.1 | async-start | bytes 163840 | tf_op jit(solution)/shard_map/all_to_all | solution.py:58
  31.4 40.3 %copy-start.2 = (f32[128,1024]{1,0:T(8,128)}, f32[128,1024]{1,0:T(8,128)S(1)}, u32[]{:S(2)}) copy-start(f32[128,1024]{1,0:T(8,128)S(1)} %get-tuple-element.14) | copy-start | bytes 1572868
  180.9 11.6 %all-to-all-start.4 = ((bf16[1,1,8,40,128]{4,3,1,0,2:T(8,128)(2,1)}), bf16[1,1,8,40,128]{4,3,1,0,2:T(8,128)(2,1)S(1)}, u32[]{:S(2)}, u32[]{:S(2)}) async-start(bf16[1,1,8,40,128]{4,3,1,0,2:T(8,128)(2,1)} %fusion.7), calls=%async_computation.4 | async-start | bytes 163840 | tf_op jit(solution)/shard_map/all_to_all | solution.py:38
where the time goes:
time: 195 us; the launch traced here: 194 us
  blocking collectives  139 us (71%)
  waiting for transfers between devices  19.4 us (10%)
  starting transfers between devices  15.3 us (8%)
  matrix products  9.88 us (5%)
  between operations  4.83 us (2%)
  local copies, waits for them, and re-layouts  4.13 us (2%)
    psum x3, blocking collectives, squares(): return lax.psum(jnp.sum(field * field), ('tile', 'freq'))  116 us
    all_to_all x2, waiting for transfers between devices, adjoint(): lax.all_to_all(coeffs, 'tile', split_axis=2, concat_axis=1, tiled=True)  12.7 us
    all_to_all x2, starting transfers between devices, adjoint(): lax.all_to_all(coeffs, 'tile', split_axis=2, concat_axis=1, tiled=True)  11.8 us
    all_to_all x1, blocking collectives, adjoint(): lax.all_to_all(coeffs, 'tile', split_axis=2, concat_axis=1, tiled=True)  11.3 us
    all_to_all x1, blocking collectives, local(): lax.all_to_all(forward_coeffs, 'tile', split_axis=1, concat_axis=2, tiled...  11.3 us
    all_to_all x1, waiting for transfers between devices, local(): lax.all_to_all(forward_coeffs, 'tile', split_axis=1, concat_axis=2, tiled...  6.74 us
    unnamed x14, local copies, waits for them, and re-layouts  3.95 us
  transfers between devices with their start and end apart: 3, of which 3 were waited for; matrix products, arithmetic and copies ran while one was open for 1% of the time, Pallas kernels for 0%

commit v1 on v0

--- a/solution.py
+++ b/solution.py
@@ -4,6 +4,13 @@
 from jax.sharding import PartitionSpec as P
 
 ITERS = 2
+
+
+def trade_parts(value, mesh_axis, split, join):
+    size = lax.axis_size(mesh_axis)
+    shards = jnp.stack(jnp.split(value, size, axis=split), axis=0)
+    shards = lax.all_to_all(shards, mesh_axis, split_axis=0, concat_axis=0)
+    return jnp.concatenate(shards, axis=join)
 
 
 def local(u_tiles, v_tiles, tile_ranks, recorded):
@@ -34,9 +41,7 @@
     def adjoint(field):
         rounded = field.astype(jnp.bfloat16).reshape(count_freq, tile_dev, width, traces)
         coeffs = row_coeffs(rounded)
-        image = apply_cols_part(
-            lax.all_to_all(coeffs, "tile", split_axis=2, concat_axis=1, tiled=True)
-        )
+        image = apply_cols_part(trade_parts(coeffs, "tile", 2, 1))
         return image.reshape(count_freq, tile_dev * width, traces)
 
     def squares(field):

time: 195 us -> 203 us (1.041)
  local copies, waits for them, and re-layouts: 4.13 us -> 13.8 us
    unnamed x14 -> x35, local copies, waits for them, and re-layouts: 3.95 us -> 12.4 us
where the time goes in v1:
time: 203 us; the launch traced here: 202 us
  blocking collectives  139 us (68%)
  waiting for transfers between devices  19.4 us (10%)
  starting transfers between devices  15.3 us (8%)
  local copies, waits for them, and re-layouts  13.8 us (7%)
  matrix products  8.62 us (4%)
  between operations  4.88 us (2%)
    psum x3, blocking collectives, squares(): return lax.psum(jnp.sum(field * field), ('tile', 'freq'))  116 us
    all_to_all x2, waiting for transfers between devices, trade_parts(): shards = lax.all_to_all(shards, mesh_axis, split_axis=0, concat_axis=0)  12.7 us
    unnamed x35, local copies, waits for them, and re-layouts  12.4 us
    all_to_all x2, starting transfers between devices, trade_parts(): shards = lax.all_to_all(shards, mesh_axis, split_axis=0, concat_axis=0)  11.8 us
    all_to_all x1, blocking collectives, local(): lax.all_to_all(forward_coeffs, 'tile', split_axis=1, concat_axis=2, tiled...  11.3 us
    all_to_all x1, blocking collectives, trade_parts(): shards = lax.all_to_all(shards, mesh_axis, split_axis=0, concat_axis=0)  11.3 us
    all_to_all x1, waiting for transfers between devices, local(): lax.all_to_all(forward_coeffs, 'tile', split_axis=1, concat_axis=2, tiled...  6.74 us
  transfers between devices with their start and end apart: 3, of which 3 were waited for; matrix products, arithmetic and copies ran while one was open for 1% of the time, Pallas kernels for 0%

profile of v1, /device:TPU:0, one launch (start us, length us, event | category | flops | bytes accessed | tf_op | source)
XLA Modules:
  0.0 202.3 jit_solution(17460094858374889610)
XLA Ops:
  0.7 0.7 copy-done.4
  1.5 1.6 fusion.9
  3.1 0.6 constant_dynamic-update-slice_fusion.7
  3.7 0.6 constant_dynamic-update-slice_fusion.6
  7.9 7.3 %all-to-all-start = ((bf16[8,1,1,1,40,128]{5,4,3,2,1,0:T(8,128)(2,1)}), bf16[8,1,1,1,40,128]{5,4,3,2,1,0:T(8,128)(2,1)S(1)}, u32[]{:S(2)}, u32[]{:S(2)}) async-start(bf16[8,1,1,1,40,128]{5,4,3,2,1,0:T(8,128)(2,1)} %constant_dynamic-update-slice_fusion), calls=%async_computation | async-start | bytes 163840 | tf_op jit(solution)/shard_map/all_to_all | solution.py:12
  15.4 6.8 %all-to-all-done = bf16[8,1,1,1,40,128]{5,4,3,2,1,0:T(8,128)(2,1)S(1)} async-done(((bf16[8,1,1,1,40,128]{5,4,3,2,1,0:T(8,128)(2,1)}), bf16[8,1,1,1,40,128]{5,4,3,2,1,0:T(8,128)(2,1)S(1)}, u32[]{:S(2)}, u32[]{:S(2)}) %all-to-all-start) | async-done | bytes 81952 | tf_op jit(solution)/shard_map/all_to_all | solution.py:12
  22.2 1.0 multiply_reduce_fusion.3
  23.2 1.0 fusion.10
  24.1 3.5 %all-to-all-start.1 = ((bf16[1,8,1,40,128]{4,3,2,0,1:T(8,128)(2,1)}), bf16[1,8,1,40,128]{4,3,2,0,1:T(8,128)(2,1)S(1)}, u32[]{:S(2)}, u32[]{:S(2)}) async-start(bf16[1,8,1,40,128]{4,3,2,0,1:T(8,128)(2,1)} %fusion.10), calls=%async_computation.1 | async-start | bytes 163840 | tf_op jit(solution)/shard_map/all_to_all | solution.py:63
  27.9 6.7 %all-to-all-done.1 = bf16[1,8,1,40,128]{4,3,2,0,1:T(8,128)(2,1)S(1)} async-done(((bf16[1,8,1,40,128]{4,3,2,0,1:T(8,128)(2,1)}), bf16[1,8,1,40,128]{4,3,2,0,1:T(8,128)(2,1)S(1)}, u32[]{:S(2)}, u32[]{:S(2)}) %all-to-all-start.1) | async-done | bytes 81952 | tf_op jit(solution)/shard_map/all_to_all | solution.py:63
  34.6 1.0 multiply_reduce_fusion.2
  35.6 38.6 %all-reduce = (f32[]{:T(128)}, f32[]{:T(128)}) all-reduce(f32[]{:T(128)} %get-tuple-element.11, f32[]{:T(128)} %get-tuple-element.13), channel_id=1, replica_groups=mesh['tile'=8,'freq'=4] {'tile','freq'}, use_global_device_ids=true, to_apply=%region_1.0 | all-reduce | flops 2 | bytes 16 | tf_op jit(solution)/shard_map/psum | solution.py:48
  76.0 11.3 %all_to_all.33 = bf16[8,1,1,1,40,128]{5,4,3,2,1,0:T(8,128)(2,1)S(1)} all-to-all(bf16[8,1,1,1,40,128]{5,4,3,2,1,0:T(8,128)(2,1)S(1)} %constant_dynamic-update-slice_fusion.8), channel_id=1, replica_groups=mesh['tile'=8,'freq'=4] {'tile'}, dimensions={0} | all-to-all | bytes 163840 | tf_op jit(solution)/shard_map/all_to_all | solution.py:12
  87.4 1.0 multiply_reduce_fusion.1
  88.4 38.6 %psum.30 = f32[]{:T(128)} all-reduce(f32[]{:T(128)} %get-tuple-element.15), channel_id=1, replica_groups=mesh['tile'=8,'freq'=4] {'tile','freq'}, use_global_device_ids=true, to_apply=%region_5.0 | all-reduce | flops 1 | bytes 8 | tf_op jit(solution)/shard_map/psum | solution.py:48
  128.7 11.3 %all_to_all.34 = bf16[1,8,1,40,128]{4,3,2,0,1:T(8,128)(2,1)S(1)} all-to-all(bf16[1,8,1,40,128]{4,3,2,0,1:T(8,128)(2,1)S(1)} %fusion.11), channel_id=1, replica_groups=mesh['tile'=8,'freq'=4] {'tile'}, dimensions={1} | all-to-all | bytes 163840 | tf_op jit(solution)/shard_map/all_to_all | solution.py:63
  140.1 1.7 multiply_reduce_fusion
  141.8 38.7 %psum.31 = f32[]{:T(128)} all-reduce(f32[]{:T(128)} %get-tuple-element.17), channel_id=1, replica_groups=mesh['tile'=8,'freq'=4] {'tile','freq'}, use_global_device_ids=true, to_apply=%region_7.0 | all-reduce | flops 1 | bytes 8 | tf_op jit(solution)/shard_map/psum | solution.py:48
  181.9 1.3 bitcast_subtract_fusion
  183.6 1.0 copy.19
  189.4 4.5 %all-to-all-start.4 = ((bf16[8,1,1,1,40,128]{5,4,3,2,1,0:T(8,128)(2,1)}), bf16[8,1,1,1,40,128]{5,4,3,2,1,0:T(8,128)(2,1)S(1)}, u32[]{:S(2)}, u32[]{:S(2)}) async-start(bf16[8,1,1,1,40,128]{5,4,3,2,1,0:T(8,128)(2,1)} %constant_dynamic-update-slice_fusion.16), calls=%async_computation.4 | async-start | bytes 163840 | tf_op jit(solution)/shard_map/all_to_all | solution.py:12
  194.0 1.0 copy.18
  195.0 5.9 %all-to-all-done.4 = bf16[8,1,1,1,40,128]{5,4,3,2,1,0:T(8,128)(2,1)S(1)} async-done(((bf16[8,1,1,1,40,128]{5,4,3,2,1,0:T(8,128)(2,1)}), bf16[8,1,1,1,40,128]{5,4,3,2,1,0:T(8,128)(2,1)S(1)}, u32[]{:S(2)}, u32[]{:S(2)}) %all-to-all-start.4) | async-done | bytes 81952 | tf_op jit(solution)/shard_map/all_to_all | solution.py:12
  201.3 1.0 copy.20
  (41 shorter events, 10.5 us)
Async XLA Ops:
  0.6 21.5 %copy-start = (bf16[1,8,1,40,1024]{4,3,2,1,0:T(8,128)(2,1)S(1)}, bf16[1,8,1,40,1024]{4,3,2,1,0:T(8,128)(2,1)}, u32[]{:S(2)}) copy-start(bf16[1,8,1,40,1024]{4,3,2,1,0:T(8,128)(2,1)} %param.5) | copy-start | bytes 1966084
  0.6 0.8 copy-start.4
  7.9 14.3 %all-to-all-start = ((bf16[8,1,1,1,40,128]{5,4,3,2,1,0:T(8,128)(2,1)}), bf16[8,1,1,1,40,128]{5,4,3,2,1,0:T(8,128)(2,1)S(1)}, u32[]{:S(2)}, u32[]{:S(2)}) async-start(bf16[8,1,1,1,40,128]{5,4,3,2,1,0:T(8,128)(2,1)} %constant_dynamic-update-slice_fusion), calls=%async_computation | async-start | bytes 163840 | tf_op jit(solution)/shard_map/all_to_all | solution.py:12
  23.2 4.5 %copy-start.3 = (f32[1,1024,128]{2,1,0:T(8,128)S(1)}, f32[1,1024,128]{2,1,0:T(8,128)}, u32[]{:S(2)}) copy-start(f32[1,1024,128]{2,1,0:T(8,128)} %param.7) | copy-start | bytes 1572868
  24.1 10.5 %copy-start.1 = (bf16[1,1,8,40,1024]{4,3,2,1,0:T(8,128)(2,1)S(1)}, bf16[1,1,8,40,1024]{4,3,2,1,0:T(8,128)(2,1)}, u32[]{:S(2)}) copy-start(bf16[1,1,8,40,1024]{4,3,2,1,0:T(8,128)(2,1)} %param.4) | copy-start | bytes 1966084
  24.1 10.4 %all-to-all-start.1 = ((bf16[1,8,1,40,128]{4,3,2,0,1:T(8,128)(2,1)}), bf16[1,8,1,40,128]{4,3,2,0,1:T(8,128)(2,1)S(1)}, u32[]{:S(2)}, u32[]{:S(2)}) async-start(bf16[1,8,1,40,128]{4,3,2,0,1:T(8,128)(2,1)} %fusion.10), calls=%async_computation.1 | async-start | bytes 163840 | tf_op jit(solution)/shard_map/all_to_all | solution.py:63
  35.6 40.3 %copy-start.2 = (f32[128,1024]{1,0:T(8,128)}, f32[128,1024]{1,0:T(8,128)S(1)}, u32[]{:S(2)}) copy-start(f32[128,1024]{1,0:T(8,128)S(1)} %get-tuple-element.14) | copy-start | bytes 1572868
  189.4 11.6 %all-to-all-start.4 = ((bf16[8,1,1,1,40,128]{5,4,3,2,1,0:T(8,128)(2,1)}), bf16[8,1,1,1,40,128]{5,4,3,2,1,0:T(8,128)(2,1)S(1)}, u32[]{:S(2)}, u32[]{:S(2)}) async-start(bf16[8,1,1,1,40,128]{5,4,3,2,1,0:T(8,128)(2,1)} %constant_dynamic-update-slice_fusion.16), calls=%async_computation.4 | async-start | bytes 163840 | tf_op jit(solution)/shard_map/all_to_all | solution.py:12
